TPU v7x, 32 devices: a whole 2x2x4 slice. The times are simulated.
32 devices in a mesh: grp: 2 (over y), mon: 4 (over z), pair: 2 (over x), sub: 2 (over core).
Axes of the slice: x: 2, y: 2, z: 4, core: 2. Of those that a mesh axis runs over, the one named last changes fastest.
Arguments:
- dfactors: bfloat16 [8192, 1024], P('mon', 'sub'), may hold values from -0.5 to 0.5
- block_mask: int32 [64, 1024], P('mon', 'sub'), may hold values 0 or 1
- base_flow: float32 [8192], P('mon'), may hold values from -5 to 5
- branch_row: int32 [1024], replicated, may hold values from 0 to 8191, as said below
- pair_slots: int32 [3072, 2], P(('grp', 'pair')), parts along dimension 0, may hold values from 0 to 1023, as said below
- pair_counts: int32 [4], P(('grp', 'pair')), parts along dimension 0, may hold values from 1 to 768, 1024 in all
Outputs:
- post_flows: bfloat16 [8192, 3072], P(('mon', 'sub'), ('grp', 'pair')), parts along dimension 1
There are 2 independent parts, one for each index of `grp`. A program takes and returns all parts, laid end to end along the dimension named above; an argument that names none is the same for every part. Nothing has to cross between parts.
Inputs may be any that keep to these rules, and one draw needn't show every extreme that they name: `branch_row`: all entries distinct. `pair_slots`: the two candidates of a slot differ; empty slots hold valid pairs too. `pair_counts`: the counts sum to 1024; an owner's live slots are its first ones.
All inputs are finite; a program needn't handle non-finite values. No bound on the sum of `block_mask` or of `pair_counts` on one device may be relied on, other than what follows from the above.
Results may differ from a plain program's by a relative error of at most 0.004.
Values may be sent and summed in bfloat16 or wider, within the bound.
A program may use at most 64 MiB of HBM per device.

v0:
```python
import jax
import jax.numpy as jnp
from jax import lax
from jax.sharding import PartitionSpec as P

BLOCK = 128


def build_shift(col_first, col_count, first_out, second_out, shift_first, shift_second):
    columns = col_first + jnp.arange(col_count, dtype=jnp.int32)[:, None]
    return (
        jnp.where(columns == first_out[None, :], shift_first[None, :], jnp.float32(0.0))
        + jnp.where(columns == second_out[None, :], shift_second[None, :], jnp.float32(0.0))
    ).astype(jnp.bfloat16)


def on_device(dfactors, block_mask, base_flow, branch_row, pair_slots, pair_counts):
    rows_dev, col_width = dfactors.shape
    blocks = block_mask.shape[0]
    masked = (
        dfactors.reshape(blocks, BLOCK, col_width) * block_mask.astype(jnp.bfloat16)[:, None, :]
    ).reshape(rows_dev, col_width)
    row_start = lax.axis_index("mon") * rows_dev
    sub_index = lax.axis_index("sub")
    col_start = sub_index * col_width
    sub_count = lax.axis_size("sub")
    capacity = pair_slots.shape[0]
    own_count = pair_counts[0]
    live_slot = (jnp.arange(capacity, dtype=jnp.int32) < own_count).astype(jnp.float32)
    first_out = pair_slots[:, 0]
    second_out = pair_slots[:, 1]
    first_row = branch_row[first_out]
    second_row = branch_row[second_out]

    def entry(row_ids, col_ids):
        local_row = row_ids - row_start
        local_col = col_ids - col_start
        inside = (
            (local_row >= 0) & (local_row < rows_dev) & (local_col >= 0) & (local_col < col_width)
        )
        value = masked[jnp.clip(local_row, 0, rows_dev - 1), jnp.clip(local_col, 0, col_width - 1)]
        return jnp.where(inside, value.astype(jnp.float32), jnp.float32(0.0))

    def flow_part(row_ids):
        local_row = row_ids - row_start
        inside = (local_row >= 0) & (local_row < rows_dev) & (sub_index == 0)
        return jnp.where(inside, base_flow[jnp.clip(local_row, 0, rows_dev - 1)], jnp.float32(0.0))

    cross_pair = jnp.stack([entry(first_row, second_out), entry(second_row, first_out)], axis=1)
    flow_pair = jnp.stack([flow_part(first_row), flow_part(second_row)], axis=1)
    cross_sum, flow_sum = lax.psum((cross_pair, flow_pair), ("mon", "sub"))
    cross_first = cross_sum[:, 0]
    cross_second = cross_sum[:, 1]
    flow_first = flow_sum[:, 0]
    flow_second = flow_sum[:, 1]
    determinant = 1.0 - cross_first * cross_second
    shift_first = (flow_first + cross_first * flow_second) / determinant
    shift_second = (flow_second + cross_second * flow_first) / determinant
    my_rows = rows_dev // sub_count
    shift = build_shift(col_start, col_width, first_out, second_out, shift_first, shift_second)
    delta = lax.psum_scatter(
        jnp.dot(masked, shift, preferred_element_type=jnp.float32).astype(jnp.bfloat16),
        "sub",
        scatter_dimension=0,
        tiled=True,
    ).astype(jnp.float32)
    flows_half = lax.dynamic_slice_in_dim(base_flow, sub_index * my_rows, my_rows, 0)
    post_flow = flows_half[:, None] + delta
    return (post_flow * live_slot[None, :]).astype(jnp.bfloat16)


def solution(mesh):
    return jax.shard_map(
        on_device,
        mesh=mesh,
        in_specs=(
            P("mon", "sub"),
            P("mon", "sub"),
            P("mon"),
            P(),
            P(("grp", "pair"), None),
            P(("grp", "pair")),
        ),
        out_specs=P(("mon", "sub"), ("grp", "pair")),
        check_vma=False,
    )
```

profile of v0, /device:TPU:0, one launch (start us, length us, event | category | flops | bytes accessed | tf_op | source)
XLA Modules:
  0.0 91.6 jit_solution(11011245030587319538)
XLA Ops:
  6.5 0.0 copy-start
  6.5 0.0 reduce-scatter.2.cloned.1.call-start
  6.5 0.7 fusion.14
  7.3 0.0 copy-done
  7.3 0.0 copy-start.2
  7.3 3.2 %gather_fusion.2 = s32[768]{0:T(1024)S(1)} fusion(s32[1024]{0:T(1024)S(1)} %copy-done, s32[1024]{0:T(1024)S(1)} %pad_clamp_fusion.1), kind=kCustom, calls=%fused_computation.2 | custom fusion | bytes 9216 | tf_op jit(solution)/shard_map/gather | solution.py:33
  10.5 0.0 copy-done.2
  10.5 0.1 slice_reduce_fusion.5
  10.6 0.0 copy-start.3
  10.6 3.2 %gather_fusion = s32[768]{0:T(1024)S(1)} fusion(s32[1024]{0:T(1024)S(1)} %copy-done, s32[1024]{0:T(1024)S(1)} %pad_clamp_fusion.3), kind=kCustom, calls=%fused_computation | custom fusion | bytes 9216 | tf_op jit(solution)/shard_map/gather | solution.py:32
  13.9 0.0 copy-done.3
  13.9 1.7 %bitcast_multiply_fusion = bf16[2048,512]{1,0:T(8,128)(2,1)S(1)} fusion(bf16[2048,512]{1,0:T(8,128)(2,1)} %param.6, bf16[16,512]{1,0:T(8,128)(2,1)S(1)} %convert_element_type.48), kind=kLoop, calls=%fused_computation.8 | loop fusion | flops 1048576 | bytes 4210688 | tf_op jit(solution)/shard_map/mul | solution.py:21
  15.7 0.0 copy-start.1
  15.7 6.7 %gather_fusion.4 = bf16[768]{0:T(1024)(128)(2,1)S(1)} fusion(bf16[2048,512]{1,0:T(8,128)(2,1)S(1)} %bitcast_multiply_fusion, s32[768]{0:T(1024)S(1)} %get-tuple-element.14), kind=kCustom, calls=%fused_computation.4 | custom fusion | bytes 9216 | tf_op jit(solution)/shard_map/gather | solution.py:41
  22.5 6.7 %gather_fusion.5 = bf16[768]{0:T(1024)(128)(2,1)S(1)} fusion(bf16[2048,512]{1,0:T(8,128)(2,1)S(1)} %bitcast_multiply_fusion, s32[768]{0:T(1024)S(1)} %get-tuple-element.6), kind=kCustom, calls=%fused_computation.5 | custom fusion | bytes 9216 | tf_op jit(solution)/shard_map/gather | solution.py:41
  29.2 0.0 copy-done.1
  29.2 4.5 %gather_fusion.1 = f32[768]{0:T(1024)S(1)} fusion(f32[2048]{0:T(1024)S(1)} %copy-done.1, s32[1024]{0:T(1024)S(1)} %pad_clamp_fusion.2), kind=kCustom, calls=%fused_computation.1 | custom fusion | bytes 9216 | tf_op jit(solution)/shard_map/gather | solution.py:47
  33.7 4.5 %gather_fusion.3 = f32[768]{0:T(1024)S(1)} fusion(f32[2048]{0:T(1024)S(1)} %copy-done.1, s32[1024]{0:T(1024)S(1)} %pad_clamp_fusion), kind=kCustom, calls=%fused_computation.3 | custom fusion | bytes 9216 | tf_op jit(solution)/shard_map/gather | solution.py:47
  38.3 30.3 %all-reduce = (f32[768,2]{0,1:T(2,128)S(1)}, f32[768,2]{0,1:T(2,128)S(1)}) all-reduce(f32[768,2]{0,1:T(2,128)S(1)} %pad_maximum_fusion, f32[768,2]{0,1:T(2,128)S(1)} %pad_maximum_fusion.1), channel_id=1, replica_groups=mesh['grp'=2,'mon'=4,'pair'=2,'sub'=2] {'mon','sub'}, use_global_device_ids=true, to_apply=%region_0.1 | all-reduce | flops 3072 | bytes 24576 | tf_op jit(solution)/shard_map/psum | solution.py:51
  68.6 3.6 %convolution_convert_fusion = bf16[2048,768]{1,0:T(8,128)(2,1)} fusion(bf16[2048,512]{1,0:T(8,128)(2,1)S(1)} %bitcast_multiply_fusion, f32[768]{0:T(1024)S(1)} %get-tuple-element.19, s32[768]{0:T(1024)S(1)} %get-tuple-element.8, f32[768]{0:T(1024)S(1)} %get-tuple-element.18, s32[768]{0:T(1024)S(1)} %get-tuple-element.5, s32[512]{0:T(512)S(1)} %iota_add_fusion), kind=kOutput, calls=%fused_computation.6 | convolution fusion | flops 1614544896 | bytes 5257216 | tf_op jit(solution)/shard_map/dot_general | solution.py:62
  72.2 0.0 reduce-scatter.2.cloned.1.call-update
  73.0 8.9 %reduce-scatter.2.cloned.1.call-done = bf16[1024,768]{1,0:T(8,128)(2,1)} async-done(((bf16[2048,768]{1,0:T(8,128)(2,1)}), bf16[1024,768]{1,0:T(8,128)(2,1)}) %reduce-scatter.2.cloned.1.call-update) | async-done | bytes 1572880 | tf_op jit(solution)/shard_map/reduce_scatter | solution.py:61
  81.8 3.0 %multiply_convert_fusion = bf16[1024,768]{1,0:T(8,128)(2,1)} fusion(bf16[1024,768]{1,0:T(8,128)(2,1)} %reduce-scatter.2.cloned.1.call-done, f32[768]{0:T(1024)S(1)} %fusion.12, f32[1024]{0:T(1024)S(1)} %dynamic_slice.3), kind=kLoop, calls=%fused_computation.7 | loop fusion | flops 3145728 | bytes 3152896 | tf_op jit(solution)/shard_map/convert_element_type | solution.py:69
  (20 shorter events, 0.2 us)
Async XLA Ops:
  6.5 0.8 copy-start
  6.5 75.3 %reduce-scatter.2.cloned.1.call-start = ((), (), s32[]{:S(2)}) async-start(), calls=%async_computation.1 | async-start | bytes 4718592 | tf_op jit(solution)/shard_map/reduce_scatter | solution.py:61
  7.3 3.2 %copy-start.2 = (s32[768,2]{0,1:T(2,128)S(1)}, s32[768,2]{0,1:T(2,128)}, u32[]{:S(2)}) copy-start(s32[768,2]{0,1:T(2,128)} %param.10) | copy-start | bytes 18436
  10.6 3.3 %copy-start.3 = (s32[16,512]{1,0:T(8,128)S(1)}, s32[16,512]{1,0:T(8,128)}, u32[]{:S(2)}) copy-start(s32[16,512]{1,0:T(8,128)} %param.7) | copy-start | bytes 98308
  15.7 13.6 %copy-start.1 = (f32[2048]{0:T(1024)S(1)}, f32[2048]{0:T(1024)}, u32[]{:S(2)}) copy-start(f32[2048]{0:T(1024)} %param.8) | copy-start | bytes 24580
Sparse Core Ops, SparseCore 0:
  72.4 9.3 reduce-scatter.1
where the time goes:
time: 91.9 us; the launch traced here: 91.6 us
  blocking collectives  30.3 us (33%)
  local copies, waits for them, and re-layouts  28.9 us (31%)
  between operations  14.3 us (16%)
  waiting for transfers between devices  8.88 us (10%)
  other arithmetic  5.66 us (6%)
  matrix products  3.63 us (4%)
    psum x1, blocking collectives, on_device(): cross_sum, flow_sum = lax.psum((cross_pair, flow_pair), ('mon', 'sub'))  30.3 us
    gather x2, local copies, waits for them, and re-layouts, entry(): masked[jnp.clip(local_row, 0, rows_dev - 1), jnp.clip(local_col, 0, col_w...  13.5 us
    gather x2, local copies, waits for them, and re-layouts, flow_part(): base_flow[jnp.clip(local_row, 0, rows_dev - 1)]  8.93 us
    reduce_scatter x1, waiting for transfers between devices, on_device(): lax.psum_scatter(jnp.dot(masked, shift, preferred_element_type=jnp.float3...  8.86 us
    dot_general x1, matrix products, on_device(): jnp.dot(masked, shift, preferred_element_type=jnp.float32)  3.63 us
    gather x1, local copies, waits for them, and re-layouts, on_device(): second_row = branch_row[second_out]  3.19 us
    gather x1, local copies, waits for them, and re-layouts, on_device(): first_row = branch_row[first_out]  3.19 us
    convert_element_type x1, other arithmetic, on_device(): return (post_flow * live_slot[None, :]).astype(jnp.bfloat16)  2.98 us
  transfers between devices with their start and end apart: 1, of which 1 were waited for; matrix products, arithmetic and copies ran while one was open for 0% of the time, Pallas kernels for 0%

commit v1 on v0

--- a/solution.py
+++ b/solution.py
@@ -48,7 +48,7 @@
 
     cross_pair = jnp.stack([entry(first_row, second_out), entry(second_row, first_out)], axis=1)
     flow_pair = jnp.stack([flow_part(first_row), flow_part(second_row)], axis=1)
-    cross_sum, flow_sum = lax.psum((cross_pair, flow_pair), ("mon", "sub"))
+    cross_sum, flow_sum = lax.psum(lax.psum((cross_pair, flow_pair), "sub"), "mon")
     cross_first = cross_sum[:, 0]
     cross_second = cross_sum[:, 1]
     flow_first = flow_sum[:, 0]

time: 91.9 us -> 85.3 us (0.928)
  blocking collectives: 30.3 us -> 23.7 us
    psum x1 -> x2, blocking collectives: 30.3 us -> 23.7 us  [the longest x1 20.1 us: on_device(): lax.psum(lax.psum((cross_pair, flow_pair), 'sub'), 'mon')]
where the time goes in v1:
time: 85.3 us; the launch traced here: 85.1 us
  local copies, waits for them, and re-layouts  28.9 us (34%)
  blocking collectives  23.7 us (28%)
  between operations  14.3 us (17%)
  waiting for transfers between devices  8.88 us (10%)
  other arithmetic  5.66 us (7%)
  matrix products  3.63 us (4%)
    psum x1, blocking collectives, on_device(): lax.psum(lax.psum((cross_pair, flow_pair), 'sub'), 'mon')  20.1 us
    gather x2, local copies, waits for them, and re-layouts, entry(): masked[jnp.clip(local_row, 0, rows_dev - 1), jnp.clip(local_col, 0, col_w...  13.5 us
    gather x2, local copies, waits for them, and re-layouts, flow_part(): base_flow[jnp.clip(local_row, 0, rows_dev - 1)]  8.93 us
    reduce_scatter x1, waiting for transfers between devices, on_device(): lax.psum_scatter(jnp.dot(masked, shift, preferred_element_type=jnp.float3...  8.86 us
    dot_general x1, matrix products, on_device(): jnp.dot(masked, shift, preferred_element_type=jnp.float32)  3.63 us
    psum x1, blocking collectives, on_device(): lax.psum((cross_pair, flow_pair), 'sub')  3.61 us
    gather x1, local copies, waits for them, and re-layouts, on_device(): second_row = branch_row[second_out]  3.19 us
    gather x1, local copies, waits for them, and re-layouts, on_device(): first_row = branch_row[first_out]  3.19 us
  transfers between devices with their start and end apart: 1, of which 1 were waited for; matrix products, arithmetic and copies ran while one was open for 0% of the time, Pallas kernels for 0%

profile of v1, /device:TPU:0, one launch (start us, length us, event | category | flops | bytes accessed | tf_op | source)
XLA Modules:
  0.0 85.1 jit_solution(1601626189836373448)
XLA Ops:
  6.5 0.0 copy-start
  6.5 0.0 reduce-scatter.2.cloned.1.call-start
  6.5 0.7 fusion.14
  7.3 0.0 copy-done
  7.3 0.0 copy-start.2
  7.3 3.2 %gather_fusion.2 = s32[768]{0:T(1024)S(1)} fusion(s32[1024]{0:T(1024)S(1)} %copy-done, s32[1024]{0:T(1024)S(1)} %pad_clamp_fusion.1), kind=kCustom, calls=%fused_computation.2 | custom fusion | bytes 9216 | tf_op jit(solution)/shard_map/gather | solution.py:33
  10.5 0.0 copy-done.2
  10.5 0.1 slice_reduce_fusion.5
  10.6 0.0 copy-start.3
  10.6 3.2 %gather_fusion = s32[768]{0:T(1024)S(1)} fusion(s32[1024]{0:T(1024)S(1)} %copy-done, s32[1024]{0:T(1024)S(1)} %pad_clamp_fusion.3), kind=kCustom, calls=%fused_computation | custom fusion | bytes 9216 | tf_op jit(solution)/shard_map/gather | solution.py:32
  13.9 0.0 copy-done.3
  13.9 1.7 %bitcast_multiply_fusion = bf16[2048,512]{1,0:T(8,128)(2,1)S(1)} fusion(bf16[2048,512]{1,0:T(8,128)(2,1)} %param.6, bf16[16,512]{1,0:T(8,128)(2,1)S(1)} %convert_element_type.48), kind=kLoop, calls=%fused_computation.8 | loop fusion | flops 1048576 | bytes 4210688 | tf_op jit(solution)/shard_map/mul | solution.py:21
  15.7 0.0 copy-start.1
  15.7 6.7 %gather_fusion.4 = bf16[768]{0:T(1024)(128)(2,1)S(1)} fusion(bf16[2048,512]{1,0:T(8,128)(2,1)S(1)} %bitcast_multiply_fusion, s32[768]{0:T(1024)S(1)} %get-tuple-element.14), kind=kCustom, calls=%fused_computation.4 | custom fusion | bytes 9216 | tf_op jit(solution)/shard_map/gather | solution.py:41
  22.5 6.7 %gather_fusion.5 = bf16[768]{0:T(1024)(128)(2,1)S(1)} fusion(bf16[2048,512]{1,0:T(8,128)(2,1)S(1)} %bitcast_multiply_fusion, s32[768]{0:T(1024)S(1)} %get-tuple-element.6), kind=kCustom, calls=%fused_computation.5 | custom fusion | bytes 9216 | tf_op jit(solution)/shard_map/gather | solution.py:41
  29.2 0.0 copy-done.1
  29.2 4.5 %gather_fusion.1 = f32[768]{0:T(1024)S(1)} fusion(f32[2048]{0:T(1024)S(1)} %copy-done.1, s32[1024]{0:T(1024)S(1)} %pad_clamp_fusion.2), kind=kCustom, calls=%fused_computation.1 | custom fusion | bytes 9216 | tf_op jit(solution)/shard_map/gather | solution.py:47
  33.7 4.5 %gather_fusion.3 = f32[768]{0:T(1024)S(1)} fusion(f32[2048]{0:T(1024)S(1)} %copy-done.1, s32[1024]{0:T(1024)S(1)} %pad_clamp_fusion), kind=kCustom, calls=%fused_computation.3 | custom fusion | bytes 9216 | tf_op jit(solution)/shard_map/gather | solution.py:47
  38.3 3.6 %all-reduce.1 = (f32[768,2]{0,1:T(2,128)S(1)}, f32[768,2]{0,1:T(2,128)S(1)}) all-reduce(f32[768,2]{0,1:T(2,128)S(1)} %pad_maximum_fusion, f32[768,2]{0,1:T(2,128)S(1)} %pad_maximum_fusion.1), channel_id=1, replica_groups=mesh['grp'=2,'mon'=4,'pair'=2,'sub'=2] {'sub'}, use_global_device_ids=true, to_apply=%region_0.1 | all-reduce | flops 3072 | bytes 24576 | tf_op jit(solution)/shard_map/psum | solution.py:51
  41.9 20.1 %all-reduce = (f32[768,2]{0,1:T(2,128)S(1)}, f32[768,2]{0,1:T(2,128)S(1)}) all-reduce(f32[768,2]{0,1:T(2,128)S(1)} %get-tuple-element.18, f32[768,2]{0,1:T(2,128)S(1)} %get-tuple-element.19), channel_id=1, replica_groups=mesh['grp'=2,'mon'=4,'pair'=2,'sub'=2] {'mon'}, use_global_device_ids=true, to_apply=%region_1.2 | all-reduce | flops 3072 | bytes 24576 | tf_op jit(solution)/shard_map/psum | solution.py:51
  62.0 3.6 %convolution_convert_fusion = bf16[2048,768]{1,0:T(8,128)(2,1)} fusion(bf16[2048,512]{1,0:T(8,128)(2,1)S(1)} %bitcast_multiply_fusion, f32[768]{0:T(1024)S(1)} %get-tuple-element.21, s32[768]{0:T(1024)S(1)} %get-tuple-element.8, f32[768]{0:T(1024)S(1)} %get-tuple-element.20, s32[768]{0:T(1024)S(1)} %get-tuple-element.5, s32[512]{0:T(512)S(1)} %iota_add_fusion), kind=kOutput, calls=%fused_computation.6 | convolution fusion | flops 1614544896 | bytes 5257216 | tf_op jit(solution)/shard_map/dot_general | solution.py:62
  65.7 0.0 reduce-scatter.2.cloned.1.call-update
  66.4 8.9 %reduce-scatter.2.cloned.1.call-done = bf16[1024,768]{1,0:T(8,128)(2,1)} async-done(((bf16[2048,768]{1,0:T(8,128)(2,1)}), bf16[1024,768]{1,0:T(8,128)(2,1)}) %reduce-scatter.2.cloned.1.call-update) | async-done | bytes 1572880 | tf_op jit(solution)/shard_map/reduce_scatter | solution.py:61
  75.2 3.0 %multiply_convert_fusion = bf16[1024,768]{1,0:T(8,128)(2,1)} fusion(bf16[1024,768]{1,0:T(8,128)(2,1)} %reduce-scatter.2.cloned.1.call-done, f32[768]{0:T(1024)S(1)} %fusion.12, f32[1024]{0:T(1024)S(1)} %dynamic_slice.3), kind=kLoop, calls=%fused_computation.7 | loop fusion | flops 3145728 | bytes 3152896 | tf_op jit(solution)/shard_map/convert_element_type | solution.py:69
  (20 shorter events, 0.2 us)
Async XLA Ops:
  6.5 0.8 copy-start
  6.5 68.7 %reduce-scatter.2.cloned.1.call-start = ((), (), s32[]{:S(2)}) async-start(), calls=%async_computation.1 | async-start | bytes 4718592 | tf_op jit(solution)/shard_map/reduce_scatter | solution.py:61
  7.3 3.2 %copy-start.2 = (s32[768,2]{0,1:T(2,128)S(1)}, s32[768,2]{0,1:T(2,128)}, u32[]{:S(2)}) copy-start(s32[768,2]{0,1:T(2,128)} %param.10) | copy-start | bytes 18436
  10.6 3.3 %copy-start.3 = (s32[16,512]{1,0:T(8,128)S(1)}, s32[16,512]{1,0:T(8,128)}, u32[]{:S(2)}) copy-start(s32[16,512]{1,0:T(8,128)} %param.7) | copy-start | bytes 98308
  15.7 13.6 %copy-start.1 = (f32[2048]{0:T(1024)S(1)}, f32[2048]{0:T(1024)}, u32[]{:S(2)}) copy-start(f32[2048]{0:T(1024)} %param.8) | copy-start | bytes 24580
Sparse Core Ops, SparseCore 0:
  65.8 9.3 reduce-scatter.1
